TPU v7x, 512 devices: a whole 4x4x16 slice. The times are simulated.
512 devices in a mesh: blk: 128 (over y_hi, z, x), feat: 4 (over y_lo, core).
Axes of the slice: x: 4, y: 4 (y_hi: 2, y_lo: 2; y = y_hi * 2 + y_lo), z: 16, core: 2. Of those that a mesh axis runs over, the one named last changes fastest.
Arguments:
- features: bfloat16 [256, 131072], P('feat', 'blk'), may hold values from -6 to 6
- block_values: bfloat16 [17408, 128, 128], P('blk'), may hold values from 0 to 1, as said below
- block_rows: int32 [17408], P('blk'), may hold values from 0 to 7, as said below
- block_cols: int32 [17408], P('blk'), may hold values from 0 to 1023, as said below
- block_count: int32 [128], P('blk'), may hold values from 8 to 136, as said below
- labels: int32 [131072], P(('blk', 'feat')), may hold values from 0 to 127
- weight_in: bfloat16 [256, 256], replicated, may hold values from -0.375 to 0.375
- weight_out: bfloat16 [256, 128], replicated, may hold values from -1 to 1
Outputs:
- logits: float32 [128, 131072], P(None, ('blk', 'feat'))
- grad_in: float32 [256, 256], replicated
- grad_out: float32 [256, 128], replicated
Inputs may be any that keep to these rules, and one draw needn't show every extreme that they name: The first block_count[s] slots of stripe s are its blocks; the remaining slots hold blocks that are not part of the matrix; every stripe holds its 8 diagonal blocks, and the busiest stripe fills all 136 slots. `block_rows`: block row of a slot inside its stripe. `block_cols`: every slot's block column lies within 8 blocks of its global block row, counted around the loop of 1024 block columns; the live slots of a stripe name distinct blocks. `block_values`: the matrix assembled from the live slots is symmetric: live block (r, c) is the transpose of live block (c, r).
All inputs are finite; a program needn't handle non-finite values.
Results may differ from a plain program's by a relative error of at most 0.002.
The roundings to bfloat16 on the way count: a program that leaves them out, or rounds other values in their place, can miss the bound.
Values may be sent and summed in bfloat16 or wider, within the bound.
No kernel may reach another device: no remote copies, remote signals or barrier semaphores. Data moves between devices by JAX's collectives and lax.ppermute only.
A program may use at most 64 MiB of HBM per device.

v0:
```python
import math
import jax
import jax.numpy as jnp
from jax import lax
from jax.sharding import PartitionSpec as P


def extended_2(cells, sides, width):
    for axis, dim in sides:
        count = lax.axis_size(axis)
        head = lax.slice_in_dim(cells, 0, width, axis=dim)
        tail = lax.slice_in_dim(cells, cells.shape[dim] - width, cells.shape[dim], axis=dim)
        cells = jnp.concatenate(
            [
                lax.ppermute(tail, axis, [(i, (i + 1) % count) for i in range(count)]),
                cells,
                lax.ppermute(head, axis, [((i + 1) % count, i) for i in range(count)]),
            ],
            axis=dim,
        )
    return cells


def propagate(extended, block_values, local_index, placing, precise):
    channels = extended.shape[0]
    block_size = block_values.shape[1]
    blocked = extended.reshape(channels, extended.shape[1] // block_size, block_size)
    gathered = jnp.take(blocked, local_index, axis=1)
    if precise:
        products = jnp.einsum(
            "csb,sab->csa",
            gathered,
            block_values.astype(jnp.float32),
            precision=lax.Precision.HIGHEST,
        )
    else:
        products = jnp.einsum(
            "csb,sab->csa", gathered, block_values, preferred_element_type=jnp.float32
        )
    placed = jnp.einsum("csa,sr->cra", products, placing, precision=lax.Precision.HIGHEST)
    return placed.reshape(channels, placing.shape[1] * block_size)


def activation(entry_value):
    return jax.nn.gelu(entry_value, approximate=True)


def on_device(
    features, block_values, block_rows, block_cols, block_count, labels, weight_in, weight_out
):
    device_count = lax.axis_size("blk")
    stripe_index = lax.axis_index("blk")
    block_size = block_values.shape[1]
    slot_count = block_rows.shape[0]
    stripe_rows = features.shape[1]
    stripe_blocks = stripe_rows // block_size
    reach_blocks = (slot_count // stripe_blocks - 1) // 2
    total_blocks = stripe_blocks * device_count
    local_index = jnp.mod(block_cols - (stripe_index * stripe_blocks - reach_blocks), total_blocks)
    live_slots = jnp.arange(slot_count, dtype=jnp.int32) < block_count[0]
    placing = (
        (block_rows[:, None] == jnp.arange(stripe_blocks, dtype=jnp.int32)[None, :])
        & live_slots[:, None]
    ).astype(jnp.float32)
    band_width = reach_blocks * block_size
    node_scale = 1.0 / math.sqrt(device_count * stripe_rows)
    input_ext = extended_2(features, (("blk", 1),), band_width)
    prop_in = propagate(input_ext, block_values, local_index, placing, False).astype(jnp.bfloat16)
    prop_rows_in = lax.all_to_all(prop_in, "feat", split_axis=1, concat_axis=0, tiled=True)
    pre_hidden = jnp.einsum(
        "ih,ir->hr", weight_in, prop_rows_in, preferred_element_type=jnp.float32
    )
    hidden = activation(pre_hidden).astype(jnp.bfloat16)
    hidden_cols = lax.all_to_all(hidden, "feat", split_axis=0, concat_axis=1, tiled=True)
    hidden_ext = extended_2(hidden_cols, (("blk", 1),), band_width)
    prop_hid = propagate(hidden_ext, block_values, local_index, placing, False).astype(jnp.bfloat16)
    prop_rows_hid = lax.all_to_all(prop_hid, "feat", split_axis=1, concat_axis=0, tiled=True)
    logits = jnp.einsum("hc,hr->cr", weight_out, prop_rows_hid, preferred_element_type=jnp.float32)
    class_count = weight_out.shape[1]
    shifted = logits - jnp.max(logits, axis=0, keepdims=True)
    exponent = jnp.exp(shifted)
    probability = exponent / jnp.sum(exponent, axis=0, keepdims=True)
    onehot = (labels[None, :] == jnp.arange(class_count, dtype=jnp.int32)[:, None]).astype(
        jnp.float32
    )
    dlogits = ((probability - onehot) * node_scale).astype(jnp.bfloat16)
    out_share = jnp.einsum("hr,cr->hc", prop_rows_hid, dlogits, preferred_element_type=jnp.float32)
    grad_out = lax.psum(out_share, ("blk", "feat"))
    back_rows = jnp.einsum("hc,cr->hr", weight_out, dlogits, preferred_element_type=jnp.float32)
    back_cols = lax.all_to_all(
        back_rows.astype(jnp.bfloat16), "feat", split_axis=0, concat_axis=1, tiled=True
    ).astype(back_rows.dtype)
    back_ext = extended_2(back_cols.astype(jnp.bfloat16), (("blk", 1),), band_width).astype(
        back_cols.dtype
    )
    back_prop = propagate(back_ext, block_values, local_index, placing, True)
    back_hid = lax.all_to_all(
        back_prop.astype(jnp.bfloat16), "feat", split_axis=1, concat_axis=0, tiled=True
    ).astype(back_prop.dtype)
    unused_output, pullback = jax.vjp(activation, pre_hidden)
    grad_pre = pullback(back_hid)[0].astype(jnp.bfloat16)
    in_share = jnp.einsum("ir,hr->ih", prop_rows_in, grad_pre, preferred_element_type=jnp.float32)
    grad_in = lax.psum(in_share, ("blk", "feat"))
    return (logits, grad_in, grad_out)


def solution(mesh):
    placed = (
        P("feat", "blk"),
        P("blk", None, None),
        P("blk"),
        P("blk"),
        P("blk"),
        P(("blk", "feat")),
        P(),
        P(),
    )
    return jax.shard_map(
        on_device,
        mesh=mesh,
        in_specs=placed,
        out_specs=(P(None, ("blk", "feat")), P(), P()),
        check_vma=False,
    )
```

profile of v0, /device:TPU:2, one launch (start us, length us, event | category | flops | bytes accessed | tf_op | source)
XLA Modules:
  0.0 618.4 jit_solution(3650204196831870399)
XLA Ops:
  7.2 3.5 collective-permute-start
  10.7 6.3 %collective-permute-start.1 = (bf16[64,1024]{1,0:T(8,128)(2,1)}, bf16[64,1024]{1,0:T(8,128)(2,1)S(1)}, u32[]{:S(2)}, u32[]{:S(2)}) collective-permute-start(bf16[64,1024]{1,0:T(8,128)(2,1)} %param.10), channel_id=1, source_target_pairs={{4,0},{8,4},{12,8},{16,12},{20,16},{24,20},{28,24},{32,28},{36,32}... | collective-permute-start | bytes 393224 | tf_op jit(solution)/shard_map/ppermute | solution.py:17
  21.9 5.4 fusion.19
  27.3 4.0 fusion.43
  31.4 7.0 %all_to_all.80 = bf16[64,4,256]{2,0,1:T(8,128)(2,1)S(1)} all-to-all(bf16[64,4,256]{2,0,1:T(8,128)(2,1)S(1)} %copy.36), channel_id=1, replica_groups=mesh['blk'=128,'feat'=4] {'feat'}, dimensions={1} | all-to-all | bytes 262144 | tf_op jit(solution)/shard_map/all_to_all | solution.py:69
  38.7 7.0 %all_to_all.81 = bf16[4,64,256]{2,1,0:T(8,128)(2,1)S(1)} all-to-all(bf16[4,64,256]{2,1,0:T(8,128)(2,1)S(1)} %bitcast.120), channel_id=1, replica_groups=mesh['blk'=128,'feat'=4] {'feat'}, dimensions={0} | all-to-all | bytes 262144 | tf_op jit(solution)/shard_map/all_to_all | solution.py:74
  45.7 11.1 %collective-permute-start.3 = (bf16[64,1024]{1,0:T(8,128)(2,1)S(1)}, bf16[64,1024]{1,0:T(8,128)(2,1)S(1)}, u32[]{:S(2)}, u32[]{:S(2)}) collective-permute-start(bf16[64,1024]{1,0:T(8,128)(2,1)S(1)} %bitcast.116), channel_id=1, source_target_pairs={{4,0},{8,4},{12,8},{16,12},{20,16},{24,20},{28,24},{32,28},{36,32}... | collective-permute-start | bytes 393224 | tf_op jit(solution)/shard_map/ppermute | solution.py:17
  56.8 2.1 collective-permute-start.2
  59.3 10.4 %collective-permute-done.2 = bf16[64,1024]{1,0:T(8,128)(2,1)S(1)} collective-permute-done((bf16[64,1024]{1,0:T(8,128)(2,1)S(1)}, bf16[64,1024]{1,0:T(8,128)(2,1)S(1)}, u32[]{:S(2)}, u32[]{:S(2)}) %collective-permute-start.2) | collective-permute-done | bytes 131104 | tf_op jit(solution)/shard_map/ppermute | solution.py:15
  70.8 5.4 fusion.22
  76.2 4.0 fusion.40
  80.4 7.0 %all_to_all.82 = bf16[64,4,256]{2,0,1:T(8,128)(2,1)S(1)} all-to-all(bf16[64,4,256]{2,0,1:T(8,128)(2,1)S(1)} %copy.43), channel_id=1, replica_groups=mesh['blk'=128,'feat'=4] {'feat'}, dimensions={1} | all-to-all | bytes 262144 | tf_op jit(solution)/shard_map/all_to_all | solution.py:77
  87.9 7.0 %all_to_all.83 = bf16[4,64,256]{2,1,0:T(8,128)(2,1)S(1)} all-to-all(bf16[4,64,256]{2,1,0:T(8,128)(2,1)S(1)} %bitcast.121), channel_id=1, replica_groups=mesh['blk'=128,'feat'=4] {'feat'}, dimensions={0} | all-to-all | bytes 262144 | tf_op jit(solution)/shard_map/all_to_all | solution.py:90
  94.9 9.6 %collective-permute-start.5 = (bf16[64,1024]{1,0:T(8,128)(2,1)S(1)}, bf16[64,1024]{1,0:T(8,128)(2,1)S(1)}, u32[]{:S(2)}, u32[]{:S(2)}) collective-permute-start(bf16[64,1024]{1,0:T(8,128)(2,1)S(1)} %bitcast.118), channel_id=1, source_target_pairs={{4,0},{8,4},{12,8},{16,12},{20,16},{24,20},{28,24},{32,28},{36,32}... | collective-permute-start | bytes 393224 | tf_op jit(solution)/shard_map/ppermute | solution.py:17
  104.5 2.1 collective-permute-start.4
  107.1 4.3 collective-permute-done.4
  111.5 2.9 gather_fusion
  114.4 11.1 %fusion.25 = f32[64,136,128]{2,0,1:T(8,128)S(1)} fusion(bf16[136,128,128]{2,1,0:T(8,128)(2,1)} %param.11, f32[136,64,128]{2,1,0:T(8,128)} %gather_fusion, pred[136]{0:T(512)(128)(4,1)S(1)} %get-tuple-element.6), kind=kOutput, calls=%fused_computation.24 | convolution fusion | flops 1712390144 | bytes 13369480 | tf_op jit(solution)/shard_map/csb,sab->csa/dot_general | solution.py:30
  125.4 4.0 fusion.37
  130.2 3.3 all-to-all-start.4
  134.5 3.7 all-to-all-done.4
  139.3 469.0 %all-reduce.3.cloned.1.call-done = (f32[256,256]{1,0:T(8,128)}, f32[256,128]{1,0:T(8,128)}) async-done(((f32[256,256]{1,0:T(8,128)}, f32[256,128]{1,0:T(8,128)}), (f32[256,256]{1,0:T(8,128)}, f32[256,128]{1,0:T(8,128)})) %all-reduce.3.cloned.1.call-update) | async-done | bytes 393232 | tf_op jit(solution)/shard_map/psum | solution.py:103
  608.3 1.7 copy.84
  610.0 1.6 copy.85
  (49 shorter events, 9.8 us)
Async XLA Ops:
  7.2 31.2 %copy-start = (bf16[256,256]{1,0:T(8,128)(2,1)S(1)}, bf16[256,256]{1,0:T(8,128)(2,1)}, u32[]{:S(2)}) copy-start(bf16[256,256]{1,0:T(8,128)(2,1)} %param.16) | copy-start | bytes 393220
  7.2 11.2 %collective-permute-start = (bf16[64,1024]{1,0:T(8,128)(2,1)}, bf16[64,1024]{1,0:T(8,128)(2,1)S(1)}, u32[]{:S(2)}, u32[]{:S(2)}) collective-permute-start(bf16[64,1024]{1,0:T(8,128)(2,1)} %param.10), channel_id=1, source_target_pairs={{0,4},{4,8},{8,12},{12,16},{16,20},{20,24},{24,28},{28,32},{32,36}... | collective-permute-start | bytes 393224 | tf_op jit(solution)/shard_map/ppermute | solution.py:15
  10.7 9.1 %collective-permute-start.1 = (bf16[64,1024]{1,0:T(8,128)(2,1)}, bf16[64,1024]{1,0:T(8,128)(2,1)S(1)}, u32[]{:S(2)}, u32[]{:S(2)}) collective-permute-start(bf16[64,1024]{1,0:T(8,128)(2,1)} %param.10), channel_id=1, source_target_pairs={{4,0},{8,4},{12,8},{16,12},{20,16},{24,20},{28,24},{32,28},{36,32}... | collective-permute-start | bytes 393224 | tf_op jit(solution)/shard_map/ppermute | solution.py:17
  21.9 5.4 copy-start.3
  45.7 13.6 %collective-permute-start.3 = (bf16[64,1024]{1,0:T(8,128)(2,1)S(1)}, bf16[64,1024]{1,0:T(8,128)(2,1)S(1)}, u32[]{:S(2)}, u32[]{:S(2)}) collective-permute-start(bf16[64,1024]{1,0:T(8,128)(2,1)S(1)} %bitcast.116), channel_id=1, source_target_pairs={{4,0},{8,4},{12,8},{16,12},{20,16},{24,20},{28,24},{32,28},{36,32}... | collective-permute-start | bytes 393224 | tf_op jit(solution)/shard_map/ppermute | solution.py:17
  56.8 12.9 %collective-permute-start.2 = (bf16[64,1024]{1,0:T(8,128)(2,1)S(1)}, bf16[64,1024]{1,0:T(8,128)(2,1)S(1)}, u32[]{:S(2)}, u32[]{:S(2)}) collective-permute-start(bf16[64,1024]{1,0:T(8,128)(2,1)S(1)} %bitcast.117), channel_id=1, source_target_pairs={{0,4},{4,8},{8,12},{12,16},{16,20},{20,24},{24,28},{28,32},{32,36}... | collective-permute-start | bytes 393224 | tf_op jit(solution)/shard_map/ppermute | solution.py:15
  76.2 11.2 %copy-start.2 = (bf16[256,128]{1,0:T(8,128)(2,1)S(1)}, bf16[256,128]{1,0:T(8,128)(2,1)}, u32[]{:S(2)}) copy-start(bf16[256,128]{1,0:T(8,128)(2,1)} %param.17) | copy-start | bytes 196612
  76.2 11.5 %copy-start.4 = (s32[256]{0:T(256)S(1)}, s32[256]{0:T(256)}, u32[]{:S(2)}) copy-start(s32[256]{0:T(256)} %param.15) | copy-start | bytes 3076
  87.6 46.0 %copy-start.1 = (f32[256,128]{0,1:T(8,128)}, f32[256,128]{0,1:T(8,128)S(1)}, u32[]{:S(2)}) copy-start(f32[256,128]{0,1:T(8,128)S(1)} %get-tuple-element.11) | copy-start | bytes 393220
  94.9 12.2 %collective-permute-start.5 = (bf16[64,1024]{1,0:T(8,128)(2,1)S(1)}, bf16[64,1024]{1,0:T(8,128)(2,1)S(1)}, u32[]{:S(2)}, u32[]{:S(2)}) collective-permute-start(bf16[64,1024]{1,0:T(8,128)(2,1)S(1)} %bitcast.118), channel_id=1, source_target_pairs={{4,0},{8,4},{12,8},{16,12},{20,16},{24,20},{28,24},{32,28},{36,32}... | collective-permute-start | bytes 393224 | tf_op jit(solution)/shard_map/ppermute | solution.py:17
  104.5 6.9 %collective-permute-start.4 = (bf16[64,1024]{1,0:T(8,128)(2,1)S(1)}, bf16[64,1024]{1,0:T(8,128)(2,1)S(1)}, u32[]{:S(2)}, u32[]{:S(2)}) collective-permute-start(bf16[64,1024]{1,0:T(8,128)(2,1)S(1)} %bitcast.119), channel_id=1, source_target_pairs={{0,4},{4,8},{8,12},{12,16},{16,20},{20,24},{24,28},{28,32},{32,36}... | collective-permute-start | bytes 393224 | tf_op jit(solution)/shard_map/ppermute | solution.py:15
  130.2 7.9 %all-to-all-start.4 = ((bf16[64,4,256]{2,0,1:T(8,128)(2,1)}), bf16[64,4,256]{2,0,1:T(8,128)(2,1)S(1)}, u32[]{:S(2)}, u32[]{:S(2)}) async-start(bf16[64,4,256]{2,0,1:T(8,128)(2,1)} %copy.50), calls=%async_computation.4 | async-start | bytes 262144 | tf_op jit(solution)/shard_map/all_to_all | solution.py:97
  133.6 474.8 %all-reduce.3.cloned.1.call-start = ((), (), s32[]{:S(2)}) async-start(), calls=%async_computation.5 | async-start | bytes 786432 | tf_op jit(solution)/shard_map/psum | solution.py:103
Sparse Core Ops, SparseCore 0:
  140.4 467.8 all-reduce.2
where the time goes:
time: 619 us; the launch traced here: 618 us
  waiting for transfers between devices  489 us (79%)
  starting transfers between devices  38.2 us (6%)
  matrix products  36.4 us (6%)
  blocking collectives  28 us (5%)
  between operations  15 us (2%)
  local copies, waits for them, and re-layouts  9.57 us (2%)
    psum x1, waiting for transfers between devices, on_device(): grad_in = lax.psum(in_share, ('blk', 'feat'))  469 us
    ppermute x3, starting transfers between devices, extended_2(): lax.ppermute(head, axis, [((i + 1) % count, i) for i in range(count)])  27.1 us
    ppermute x3, waiting for transfers between devices, extended_2(): lax.ppermute(tail, axis, [(i, (i + 1) % count) for i in range(count)])  14.8 us
  transfers between devices with their start and end apart: 8, of which 7 were waited for; matrix products, arithmetic and copies ran while one was open for 0% of the time, Pallas kernels for 0%

commit v1 on v0

--- a/solution.py
+++ b/solution.py
@@ -100,7 +100,7 @@
     unused_output, pullback = jax.vjp(activation, pre_hidden)
     grad_pre = pullback(back_hid)[0].astype(jnp.bfloat16)
     in_share = jnp.einsum("ir,hr->ih", prop_rows_in, grad_pre, preferred_element_type=jnp.float32)
-    grad_in = lax.psum(in_share, ("blk", "feat"))
+    grad_in = lax.psum(lax.psum(in_share, "feat"), "blk")
     return (logits, grad_in, grad_out)
 
 

time: 619 us -> 1880 us (3.04)
  the two profiles are of different devices: /device:TPU:2 before, /device:TPU:24 now
where the time goes in v1:
time: 1880 us
  waiting for transfers between devices  1750 us (93%)
  matrix products  36.4 us (2%)
  starting transfers between devices  34.5 us (2%)
  blocking collectives  33 us (2%)
    psum x2, waiting for transfers between devices, on_device(): grad_in = lax.psum(lax.psum(in_share, 'feat'), 'blk')  1260 us
    psum x1, waiting for transfers between devices, on_device(): grad_out = lax.psum(out_share, ('blk', 'feat'))  462 us
  transfers between devices with their start and end apart: 9, of which 9 were waited for; matrix products, arithmetic and copies ran while one was open for 0% of the time, Pallas kernels for 0%

profile of v1, /device:TPU:24, one launch (start us, length us, event | category | flops | bytes accessed | tf_op | source)
XLA Modules:
  0.0 1876.1 jit_solution(6624902987727202647)
XLA Ops:
  7.2 3.4 collective-permute-start
  10.6 12.8 collective-permute-start.1
  28.5 5.4 fusion.19
  33.9 4.0 fusion.43
  38.0 6.1 all_to_all.80
  44.4 7.0 all_to_all.81
  51.4 10.0 collective-permute-start.3
  61.4 2.1 collective-permute-start.2
  64.2 9.8 collective-permute-done.2
  75.1 5.4 fusion.22
  80.5 4.0 fusion.40
  84.7 6.3 all_to_all.82
  91.5 7.0 all_to_all.83
  98.5 2.1 collective-permute-start.5
  100.6 4.0 collective-permute-start.4
  105.7 7.6 collective-permute-done.4
  113.4 2.9 gather_fusion
  116.3 11.1 fusion.25
  127.4 4.0 fusion.37
  131.5 6.7 all_to_all.84
  140.3 39.5 %all-reduce.4.cloned.1.call-done = f32[256,256]{1,0:T(8,128)} async-done(((f32[256,256]{1,0:T(8,128)}), f32[256,256]{1,0:T(8,128)}) %all-reduce.4.cloned.1.call-update) | async-done | bytes 262160 | tf_op jit(solution)/shard_map/psum | solution.py:103
  179.8 461.9 %all-reduce.8.cloned.1.call-done = f32[256,128]{1,0:T(8,128)} async-done(((f32[256,128]{1,0:T(8,128)}), f32[256,128]{1,0:T(8,128)}) %all-reduce.8.cloned.1.call-update) | async-done | bytes 131088 | tf_op jit(solution)/shard_map/psum | solution.py:88
  641.8 1224.5 %all-reduce.6.cloned.1.call-done = f32[256,256]{1,0:T(8,128)} async-done(((f32[256,256]{1,0:T(8,128)}), f32[256,256]{1,0:T(8,128)}) %all-reduce.6.cloned.1.call-update) | async-done | bytes 262160 | tf_op jit(solution)/shard_map/psum | solution.py:103
  1866.3 1.7 copy.85
  (54 shorter events, 12.2 us)
Async XLA Ops:
  7.2 36.9 %copy-start = (bf16[256,256]{1,0:T(8,128)(2,1)S(1)}, bf16[256,256]{1,0:T(8,128)(2,1)}, u32[]{:S(2)}) copy-start(bf16[256,256]{1,0:T(8,128)(2,1)} %param.16) | copy-start | bytes 393220
  7.2 172.6 %all-reduce.4.cloned.1.call-start = ((), (), s32[]{:S(2)}) async-start(), calls=%async_computation.5 | async-start | bytes 524288 | tf_op jit(solution)/shard_map/psum | solution.py:103
  7.2 18.0 collective-permute-start
  10.6 15.8 collective-permute-start.1
  28.5 5.4 copy-start.3
  51.4 12.8 collective-permute-start.3
  61.4 12.6 collective-permute-start.2
  80.5 10.5 copy-start.2
  80.5 10.8 copy-start.4
  91.2 48.2 %copy-start.1 = (f32[256,128]{0,1:T(8,128)}, f32[256,128]{0,1:T(8,128)S(1)}, u32[]{:S(2)}) copy-start(f32[256,128]{0,1:T(8,128)S(1)} %get-tuple-element.9) | copy-start | bytes 393220
  98.5 7.2 collective-permute-start.5
  100.6 12.7 collective-permute-start.4
  139.3 502.4 %all-reduce.8.cloned.1.call-start = ((), (), s32[]{:S(2)}) async-start(), calls=%async_computation.7 | async-start | bytes 262144 | tf_op jit(solution)/shard_map/psum | solution.py:88
  140.3 1726.0 %all-reduce.6.cloned.1.call-start = ((), (), s32[]{:S(2)}) async-start(), calls=%async_computation.6 | async-start | bytes 524288 | tf_op jit(solution)/shard_map/psum | solution.py:103
Sparse Core Ops, SparseCore 0:
  139.5 40.2 all-reduce.3
  185.8 455.8 all-reduce.7
  644.7 1221.5 all-reduce.5
